TPU v7x, 512 devices: a whole 4x8x8 slice. The times are simulated.
512 devices in a mesh: box: 64 (over y, x, core), samp: 8 (over z).
Axes of the slice: x: 4, y: 8, z: 8, core: 2. Of those that a mesh axis runs over, the one named last changes fastest.
Arguments:
- currents: bfloat16 [2048, 8, 128], P(('box', 'samp')), may hold values from -6 to 6
- radiation: bfloat16 [2048, 2, 2, 512, 128], P(('box', 'samp')), may hold values from -0.1875 to 0.1875
- near_blocks: bfloat16 [2048, 8, 2, 128, 128], P(('box', 'samp')), may hold values from -0.125 to 0.125
- near_src: int32 [2048, 8], P(('box', 'samp')), may hold values from 0 to 2047, as said below
- leaf_parent: int32 [2048], P('box'), may hold values from 0 to 1023, as said below
- leaf_shift: int32 [2048], P('box'), may hold values from 0 to 7
- shift_table: bfloat16 [8, 2, 8192], P(None, None, 'samp'), may hold values from -4 to 4
- interp_idx: int32 [64, 2], P('samp'), may hold values from 0 to 3, as said below
- interp_val: bfloat16 [64, 2, 128, 128], P('samp'), may hold values from -0.375 to 0.375
- top_src: int32 [1024, 16], P('box'), may hold values from 0 to 1023, as said below
- top_disp: int32 [1024, 16], P('box'), may hold values from 0 to 31
- trans_table: bfloat16 [32, 2, 8192], P(None, None, 'samp'), may hold values from -1 to 1
Outputs:
- matvec: float32 [2048, 8, 128], P(('box', 'samp'))
Inputs may be any that keep to these rules, and one draw needn't show every extreme that they name: `near_src`: entry 0 of a leaf's row is the leaf itself; every entry lies in the 4 leaves of the leaf's own device or of the devices just before and after it in box+samp order (leaves numbered box-major), and these ends are reached. `leaf_parent`: the parent of leaf l lies in its box group: its value divided by 16 equals l divided by 32. `interp_idx`: the 2 entries of a row differ. `top_src`: a source of top box t is another box of t's group (t // 16), or one of the last 8 boxes of the group before it, or one of the first 8 boxes of the group after it; both rims are reached.
All inputs are finite; a program needn't handle non-finite values.
Results may differ from a plain program's by a relative error of at most 0.013.
Values may be sent and summed in bfloat16 or wider, within the bound.
A program may use at most 64 MiB of HBM per device.

v0:
```python
import jax
import jax.numpy as jnp
from jax import lax
from jax.sharding import PartitionSpec as P

HIGHEST = lax.Precision.HIGHEST


def with_halo(cells, sides, width):
    for axis, dim in sides:
        count = lax.axis_size(axis)
        ends = count - 1
        head = lax.slice_in_dim(cells, 0, width, axis=dim)
        tail = lax.slice_in_dim(cells, cells.shape[dim] - width, cells.shape[dim], axis=dim)
        cells = jnp.concatenate(
            [
                lax.ppermute(tail, axis, [(i, (i + 1) % count) for i in range(ends)]),
                cells,
                lax.ppermute(head, axis, [((i + 1) % count, i) for i in range(ends)]),
            ],
            axis=dim,
        )
    return cells


def complex_mul(a_real, a_imag, b_real, b_imag):
    return (a_real * b_real - a_imag * b_imag, a_real * b_imag + a_imag * b_real)


def contract(form, first_op, second_op):
    return jnp.einsum(form, first_op, second_op, preferred_element_type=jnp.float32)


def per_device(
    currents,
    radiation,
    near_blocks,
    near_src,
    leaf_parent,
    leaf_shift,
    shift_table,
    interp_idx,
    interp_val,
    top_src,
    top_disp,
    trans_table,
):
    leaf_count = currents.shape[0]
    half_comp = currents.shape[1]
    excite = half_comp // 2
    comps = 2 * half_comp
    samp_count = lax.axis_size("samp")
    group_index = lax.axis_index("box")
    first_leaf = (group_index * samp_count + lax.axis_index("samp")) * leaf_count
    top_count = top_src.shape[0]
    block_size = interp_val.shape[2]
    leaf_samples = radiation.shape[3]
    in_blocks = leaf_samples // block_size
    local_blocks = interp_val.shape[0]
    local_samples = local_blocks * block_size
    neighbours = with_halo(currents, ((("box", "samp"), 0),), leaf_count)
    rad_real = radiation[:, :, 0]
    rad_imag = radiation[:, :, 1]
    form_out = "lpqu,leu->lpeq"
    out_real = contract(form_out, rad_real, currents[:, :excite]) - contract(
        form_out, rad_imag, currents[:, excite:]
    )
    out_imag = contract(form_out, rad_real, currents[:, excite:]) + contract(
        form_out, rad_imag, currents[:, :excite]
    )
    patterns = jnp.concatenate(
        [
            out_real.reshape(leaf_count, half_comp, leaf_samples),
            out_imag.reshape(leaf_count, half_comp, leaf_samples),
        ],
        axis=1,
    ).astype(jnp.bfloat16)
    piece = lax.all_gather(patterns, "samp", axis=0, tiled=True)
    piece_rows = piece.shape[0]
    picked = piece.reshape(piece_rows, comps, in_blocks, block_size)[:, :, interp_idx, :]
    moved_rows = contract("lcbri,brki->lcbk", picked, interp_val)
    moved = moved_rows.reshape(piece_rows, comps, local_samples)
    shift_onehot = (leaf_shift[:, None] == jnp.arange(shift_table.shape[0])[None, :]).astype(
        jnp.bfloat16
    )
    shift_rows = contract("ln,nrk->lrk", shift_onehot, shift_table)
    shift_real = shift_rows[:, 0:1]
    shift_imag = shift_rows[:, 1:2]
    up_real, up_imag = complex_mul(
        moved[:, :half_comp], moved[:, half_comp:], shift_real, shift_imag
    )
    shifted = jnp.concatenate([up_real, up_imag], axis=1)
    parent_local = leaf_parent - group_index * top_count
    member = parent_local[None, :] == jnp.arange(top_count)[:, None]
    top_patterns = jnp.einsum(
        "tl,lck->tck", member.astype(jnp.float32), shifted, precision=HIGHEST
    ).astype(jnp.bfloat16)
    padded = with_halo(top_patterns, (("box", 0),), top_count)
    base_index = group_index * top_count - top_count
    disp_count = trans_table.shape[0]

    def add_entry(entry, total):
        source_rows = jnp.take(padded, top_src[:, entry] - base_index, axis=0).astype(jnp.float32)
        disp_onehot = (top_disp[:, entry][:, None] == jnp.arange(disp_count)[None, :]).astype(
            jnp.bfloat16
        )
        coeff = contract("tn,nrk->trk", disp_onehot, trans_table)
        part_real, part_imag = complex_mul(
            coeff[:, 0:1], coeff[:, 1:2], source_rows[:, :half_comp], source_rows[:, half_comp:]
        )
        return total + jnp.concatenate([part_real, part_imag], axis=1)

    incoming = lax.fori_loop(
        0, top_src.shape[1], add_entry, jnp.zeros((top_count, comps, local_samples), jnp.float32)
    ).astype(jnp.bfloat16)
    spread = contract("tl,tck->lck", member.astype(jnp.bfloat16), incoming)
    down_real, down_imag = complex_mul(
        shift_real, -shift_imag, spread[:, :half_comp], spread[:, half_comp:]
    )
    down = jnp.concatenate([down_real, down_imag], axis=1).astype(jnp.bfloat16)
    block_onehot = (interp_idx[:, :, None] == jnp.arange(in_blocks)[None, None, :]).astype(
        jnp.float32
    )
    parts = contract(
        "lcbk,brki->lcbri",
        down.reshape(leaf_count * lax.axis_size("samp"), comps, local_blocks, block_size),
        interp_val,
    )
    folded = jnp.einsum("lcbri,brq->lcqi", parts, block_onehot, precision=HIGHEST)
    far = lax.psum_scatter(
        folded.reshape(leaf_count * lax.axis_size("samp"), comps, leaf_samples).astype(
            jnp.bfloat16
        ),
        "samp",
        scatter_dimension=0,
        tiled=True,
    )
    far_real = far[:, :half_comp].reshape(leaf_count, 2, excite, leaf_samples)
    far_imag = far[:, half_comp:].reshape(leaf_count, 2, excite, leaf_samples)
    form_back = "lpqu,lpeq->leu"
    recv_real = contract(form_back, rad_real, far_real) + contract(form_back, rad_imag, far_imag)
    recv_imag = contract(form_back, rad_real, far_imag) - contract(form_back, rad_imag, far_real)
    near_rows = jnp.take(neighbours, near_src - first_leaf + leaf_count, axis=0)
    block_real = near_blocks[:, :, 0]
    block_imag = near_blocks[:, :, 1]
    form_near = "lnuv,lnev->leu"
    near_real = contract(form_near, block_real, near_rows[:, :, :excite]) - contract(
        form_near, block_imag, near_rows[:, :, excite:]
    )
    near_imag = contract(form_near, block_real, near_rows[:, :, excite:]) + contract(
        form_near, block_imag, near_rows[:, :, :excite]
    )
    return jnp.concatenate([recv_real + near_real, recv_imag + near_imag], axis=1)


def solution(mesh):
    placed = (
        P(("box", "samp"), None, None),
        P(("box", "samp"), None, None, None, None),
        P(("box", "samp"), None, None, None, None),
        P(("box", "samp"), None),
        P("box"),
        P("box"),
        P(None, None, "samp"),
        P("samp", None),
        P("samp", None, None, None),
        P("box", None),
        P("box", None),
        P(None, None, "samp"),
    )
    return jax.shard_map(
        per_device,
        mesh=mesh,
        in_specs=placed,
        out_specs=P(("box", "samp"), None, None),
        check_vma=False,
    )
```

profile of v0, /device:TPU:2, one launch (start us, length us, event | category | flops | bytes accessed | tf_op | source)
XLA Modules:
  0.0 176.0 jit_solution(13195029039709390717)
XLA Ops:
  6.6 1.8 %fusion.46 = f32[4,4,2,512]{3,1,2,0:T(4,128)S(1)} fusion(bf16[4,2,2,512,128]{4,3,2,1,0:T(8,128)(2,1)} %param.15, bf16[4,8,128]{2,1,0:T(8,128)(2,1)} %param.14), kind=kOutput, calls=%fused_computation.65 | convolution fusion | flops 4194304 | bytes 1118208 | tf_op jit(solution)/shard_map/lpqu,leu->lpeq/dot_general | solution.py:31
  8.4 1.6 fusion.44
  10.3 0.4 fusion.25
  11.1 31.6 %all_gather.3 = bf16[32,16,512]{2,1,0:T(8,128)(2,1)S(1)} all-gather(bf16[4,16,512]{2,1,0:T(8,128)(2,1)S(1)} %pad_maximum_fusion.1), channel_id=1, replica_groups=mesh['box'=64,'samp'=8] {'samp'}, dimensions={0}, use_global_device_ids=true | all-gather | bytes 589824 | tf_op jit(solution)/shard_map/all_gather | solution.py:78
  43.1 1.1 gather_fusion.1
  44.2 0.7 convolution_bitcast_fusion.1
  44.9 2.5 %copy.92 = f32[32,16,8,128]{3,2,0,1:T(8,128)} copy(f32[32,16,8,128]{3,1,0,2:T(8,128)S(1)} %convolution_bitcast_fusion.1) | data formatting | bytes 4194304 | tf_op jit(solution)/shard_map/reshape | solution.py:82
  47.4 1.7 reshape.96
  49.5 0.8 fusion.16
  50.4 1.9 %collective-permute-start = (bf16[16,16,1024]{2,0,1:T(8,128)(2,1)S(1)}, bf16[16,16,1024]{2,0,1:T(8,128)(2,1)S(1)}, u32[]{:S(2)}, u32[]{:S(2)}) collective-permute-start(bf16[16,16,1024]{2,0,1:T(8,128)(2,1)S(1)} %fusion.16), channel_id=1, source_target_pairs={{0,8},{8,16},{16,24},{24,32},{32,40},{40,48},{48,56},{56,64},{64,7... | collective-permute-start | bytes 1572872 | tf_op jit(solution)/shard_map/ppermute | solution.py:17
  52.3 3.8 %collective-permute-start.1 = (bf16[16,16,1024]{2,0,1:T(8,128)(2,1)S(1)}, bf16[16,16,1024]{2,0,1:T(8,128)(2,1)}, u32[]{:S(2)}, u32[]{:S(2)}) collective-permute-start(bf16[16,16,1024]{2,0,1:T(8,128)(2,1)S(1)} %fusion.16), channel_id=1, source_target_pairs={{8,0},{16,8},{24,16},{32,24},{40,32},{48,40},{56,48},{64,56},{72,6... | collective-permute-start | bytes 1572872 | tf_op jit(solution)/shard_map/ppermute | solution.py:19
  56.3 4.5 %collective-permute-done = bf16[16,16,1024]{2,0,1:T(8,128)(2,1)S(1)} collective-permute-done((bf16[16,16,1024]{2,0,1:T(8,128)(2,1)S(1)}, bf16[16,16,1024]{2,0,1:T(8,128)(2,1)S(1)}, u32[]{:S(2)}, u32[]{:S(2)}) %collective-permute-start) | collective-permute-done | bytes 524320 | tf_op jit(solution)/shard_map/ppermute | solution.py:17
  60.9 1.8 collective-permute-done.1
  62.6 1.2 pad_maximum_fusion
  63.8 2.0 %copy.70 = bf16[48,16,1024]{2,1,0:T(8,128)(2,1)} copy(bf16[48,16,1024]{2,0,1:T(8,128)(2,1)S(1)} %pad_maximum_fusion) | data formatting | bytes 3145728
  65.9 48.1 %while.14 = (s32[]{:T(128)}, f32[16,16,1024]{2,1,0:T(8,128)S(1)}, s32[16,16]{0,1:T(8,128)S(1)}, bf16[32,2,1024]{2,0,1:T(8,128)(2,1)S(1)}, s32[16,16]{0,1:T(8,128...) while((s32[]{:T(128)}, f32[16,16,1024]{2,1,0:T(8,128)S(1)}, ...), condition=%wide.region_1.0_spmd.clone, body=%wide.region_0.1_spmd.clone.sunk | while | flops 4195955 | bytes 8524371 | solution.py:113
  65.9 2.0 %gather_fusion = bf16[16,16,1024]{2,1,0:T(8,128)(2,1)S(1)} fusion(bf16[48,16,1024]{2,1,0:T(8,128)(2,1)} %get-tuple-element.292, s32[1024]{0:T(1024)S(1)} %pad_clamp_fusion.4), kind=kCustom, calls=%fused_computation.clone.clone.1 | custom fusion | bytes 1048640 | tf_op jit(solution)/shard_map/while/body/eval_jaxpr/jit(_take)/gather | solution.py:103
  68.9 2.0 %gather_fusion = bf16[16,16,1024]{2,1,0:T(8,128)(2,1)S(1)} fusion(bf16[48,16,1024]{2,1,0:T(8,128)(2,1)} %get-tuple-element.292, s32[1024]{0:T(1024)S(1)} %pad_clamp_fusion.4), kind=kCustom, calls=%fused_computation.clone.clone.1 | custom fusion | bytes 1048640 | tf_op jit(solution)/shard_map/while/body/eval_jaxpr/jit(_take)/gather | solution.py:103
  71.9 2.0 %gather_fusion = bf16[16,16,1024]{2,1,0:T(8,128)(2,1)S(1)} fusion(bf16[48,16,1024]{2,1,0:T(8,128)(2,1)} %get-tuple-element.292, s32[1024]{0:T(1024)S(1)} %pad_clamp_fusion.4), kind=kCustom, calls=%fused_computation.clone.clone.1 | custom fusion | bytes 1048640 | tf_op jit(solution)/shard_map/while/body/eval_jaxpr/jit(_take)/gather | solution.py:103
  74.9 2.0 %gather_fusion = bf16[16,16,1024]{2,1,0:T(8,128)(2,1)S(1)} fusion(bf16[48,16,1024]{2,1,0:T(8,128)(2,1)} %get-tuple-element.292, s32[1024]{0:T(1024)S(1)} %pad_clamp_fusion.4), kind=kCustom, calls=%fused_computation.clone.clone.1 | custom fusion | bytes 1048640 | tf_op jit(solution)/shard_map/while/body/eval_jaxpr/jit(_take)/gather | solution.py:103
  77.9 2.0 %gather_fusion = bf16[16,16,1024]{2,1,0:T(8,128)(2,1)S(1)} fusion(bf16[48,16,1024]{2,1,0:T(8,128)(2,1)} %get-tuple-element.292, s32[1024]{0:T(1024)S(1)} %pad_clamp_fusion.4), kind=kCustom, calls=%fused_computation.clone.clone.1 | custom fusion | bytes 1048640 | tf_op jit(solution)/shard_map/while/body/eval_jaxpr/jit(_take)/gather | solution.py:103
  80.9 2.0 %gather_fusion = bf16[16,16,1024]{2,1,0:T(8,128)(2,1)S(1)} fusion(bf16[48,16,1024]{2,1,0:T(8,128)(2,1)} %get-tuple-element.292, s32[1024]{0:T(1024)S(1)} %pad_clamp_fusion.4), kind=kCustom, calls=%fused_computation.clone.clone.1 | custom fusion | bytes 1048640 | tf_op jit(solution)/shard_map/while/body/eval_jaxpr/jit(_take)/gather | solution.py:103
  83.9 2.0 %gather_fusion = bf16[16,16,1024]{2,1,0:T(8,128)(2,1)S(1)} fusion(bf16[48,16,1024]{2,1,0:T(8,128)(2,1)} %get-tuple-element.292, s32[1024]{0:T(1024)S(1)} %pad_clamp_fusion.4), kind=kCustom, calls=%fused_computation.clone.clone.1 | custom fusion | bytes 1048640 | tf_op jit(solution)/shard_map/while/body/eval_jaxpr/jit(_take)/gather | solution.py:103
  86.9 2.0 %gather_fusion = bf16[16,16,1024]{2,1,0:T(8,128)(2,1)S(1)} fusion(bf16[48,16,1024]{2,1,0:T(8,128)(2,1)} %get-tuple-element.292, s32[1024]{0:T(1024)S(1)} %pad_clamp_fusion.4), kind=kCustom, calls=%fused_computation.clone.clone.1 | custom fusion | bytes 1048640 | tf_op jit(solution)/shard_map/while/body/eval_jaxpr/jit(_take)/gather | solution.py:103
  90.0 2.0 %gather_fusion = bf16[16,16,1024]{2,1,0:T(8,128)(2,1)S(1)} fusion(bf16[48,16,1024]{2,1,0:T(8,128)(2,1)} %get-tuple-element.292, s32[1024]{0:T(1024)S(1)} %pad_clamp_fusion.4), kind=kCustom, calls=%fused_computation.clone.clone.1 | custom fusion | bytes 1048640 | tf_op jit(solution)/shard_map/while/body/eval_jaxpr/jit(_take)/gather | solution.py:103
  93.0 2.0 %gather_fusion = bf16[16,16,1024]{2,1,0:T(8,128)(2,1)S(1)} fusion(bf16[48,16,1024]{2,1,0:T(8,128)(2,1)} %get-tuple-element.292, s32[1024]{0:T(1024)S(1)} %pad_clamp_fusion.4), kind=kCustom, calls=%fused_computation.clone.clone.1 | custom fusion | bytes 1048640 | tf_op jit(solution)/shard_map/while/body/eval_jaxpr/jit(_take)/gather | solution.py:103
  96.0 2.0 %gather_fusion = bf16[16,16,1024]{2,1,0:T(8,128)(2,1)S(1)} fusion(bf16[48,16,1024]{2,1,0:T(8,128)(2,1)} %get-tuple-element.292, s32[1024]{0:T(1024)S(1)} %pad_clamp_fusion.4), kind=kCustom, calls=%fused_computation.clone.clone.1 | custom fusion | bytes 1048640 | tf_op jit(solution)/shard_map/while/body/eval_jaxpr/jit(_take)/gather | solution.py:103
  99.0 2.0 %gather_fusion = bf16[16,16,1024]{2,1,0:T(8,128)(2,1)S(1)} fusion(bf16[48,16,1024]{2,1,0:T(8,128)(2,1)} %get-tuple-element.292, s32[1024]{0:T(1024)S(1)} %pad_clamp_fusion.4), kind=kCustom, calls=%fused_computation.clone.clone.1 | custom fusion | bytes 1048640 | tf_op jit(solution)/shard_map/while/body/eval_jaxpr/jit(_take)/gather | solution.py:103
  102.0 2.0 %gather_fusion = bf16[16,16,1024]{2,1,0:T(8,128)(2,1)S(1)} fusion(bf16[48,16,1024]{2,1,0:T(8,128)(2,1)} %get-tuple-element.292, s32[1024]{0:T(1024)S(1)} %pad_clamp_fusion.4), kind=kCustom, calls=%fused_computation.clone.clone.1 | custom fusion | bytes 1048640 | tf_op jit(solution)/shard_map/while/body/eval_jaxpr/jit(_take)/gather | solution.py:103
  105.0 2.0 %gather_fusion = bf16[16,16,1024]{2,1,0:T(8,128)(2,1)S(1)} fusion(bf16[48,16,1024]{2,1,0:T(8,128)(2,1)} %get-tuple-element.292, s32[1024]{0:T(1024)S(1)} %pad_clamp_fusion.4), kind=kCustom, calls=%fused_computation.clone.clone.1 | custom fusion | bytes 1048640 | tf_op jit(solution)/shard_map/while/body/eval_jaxpr/jit(_take)/gather | solution.py:103
  108.0 2.0 %gather_fusion = bf16[16,16,1024]{2,1,0:T(8,128)(2,1)S(1)} fusion(bf16[48,16,1024]{2,1,0:T(8,128)(2,1)} %get-tuple-element.292, s32[1024]{0:T(1024)S(1)} %pad_clamp_fusion.4), kind=kCustom, calls=%fused_computation.clone.clone.1 | custom fusion | bytes 1048640 | tf_op jit(solution)/shard_map/while/body/eval_jaxpr/jit(_take)/gather | solution.py:103
  111.0 2.0 %gather_fusion = bf16[16,16,1024]{2,1,0:T(8,128)(2,1)S(1)} fusion(bf16[48,16,1024]{2,1,0:T(8,128)(2,1)} %get-tuple-element.292, s32[1024]{0:T(1024)S(1)} %pad_clamp_fusion.4), kind=kCustom, calls=%fused_computation.clone.clone.1 | custom fusion | bytes 1048640 | tf_op jit(solution)/shard_map/while/body/eval_jaxpr/jit(_take)/gather | solution.py:103
  114.0 0.5 fusion.62
  115.8 0.7 convolution_bitcast_fusion
  116.5 4.0 %fusion.19 = bf16[32,16,4,128]{3,2,1,0:T(4,128)(2,1)S(1)} fusion(f32[32,16,8,2,128]{4,1,3,0,2:T(8,128)S(1)} %convolution_bitcast_fusion, s32[8,2]{0,1:T(2,128)S(1)} %copy-done.9), kind=kOutput, calls=%fused_computation.29 | convolution fusion | flops 50593856 | bytes 4718656 | tf_op jit(solution)/shard_map/lcbri,brq->lcqi/dot_general | solution.py:129
  120.6 1.0 convert_element_type.36
  121.6 3.7 %collective-permute-start.2 = (bf16[4,8,128]{2,1,0:T(8,128)(2,1)S(1)}, bf16[4,8,128]{2,1,0:T(8,128)(2,1)S(1)}, u32[]{:S(2)}, u32[]{:S(2)}) collective-permute-start(bf16[4,8,128]{2,1,0:T(8,128)(2,1)S(1)} %copy-done.4), channel_id=1, source_target_pairs={{0,1},{1,2},{2,3},{3,4},{4,5},{5,6},{6,7},{7,8},{8,9},{9,10},{10,1... | collective-permute-start | bytes 24584 | tf_op jit(solution)/shard_map/ppermute | solution.py:17
  125.3 4.6 %collective-permute-start.3 = (bf16[4,8,128]{2,1,0:T(8,128)(2,1)S(1)}, bf16[4,8,128]{2,1,0:T(8,128)(2,1)S(1)}, u32[]{:S(2)}, u32[]{:S(2)}) collective-permute-start(bf16[4,8,128]{2,1,0:T(8,128)(2,1)S(1)} %copy-done.4), channel_id=1, source_target_pairs={{1,0},{2,1},{3,2},{4,3},{5,4},{6,5},{7,6},{8,7},{9,8},{10,9},{11,1... | collective-permute-start | bytes 24584 | tf_op jit(solution)/shard_map/ppermute | solution.py:19
  130.0 1.2 collective-permute-done.3
  131.2 0.6 gather_fusion.2
  131.9 1.6 convolution_bitcast_fusion.7
  133.5 1.6 convolution_bitcast_fusion.3
  135.2 29.9 %reduce-scatter.2.cloned.1.call-done = bf16[4,16,512]{2,1,0:T(8,128)(2,1)} async-done(((bf16[32,16,512]{2,1,0:T(8,128)(2,1)}), bf16[4,16,512]{2,1,0:T(8,128)(2,1)}) %reduce-scatter.2.cloned.1.call-update) | async-done | bytes 65552 | tf_op jit(solution)/shard_map/reduce_scatter | solution.py:130
  165.0 0.8 fusion.91
  166.9 0.8 copy-done.3
  167.7 0.4 fusion.30
  168.1 0.4 fusion.27
  168.5 0.6 pad_maximum_fusion.3
  (190 shorter events, 19.1 us)
Async XLA Ops:
  6.5 37.6 %copy-start = (bf16[8,2,128,128]{3,2,1,0:T(8,128)(2,1)S(1)}, bf16[8,2,128,128]{3,2,1,0:T(8,128)(2,1)}, u32[]{:S(2)}) copy-start(bf16[8,2,128,128]{3,2,1,0:T(8,128)(2,1)} %param.22) | copy-start | bytes 1572868
  6.5 3.7 %copy-start.4 = (bf16[4,8,128]{2,1,0:T(8,128)(2,1)S(1)}, bf16[4,8,128]{2,1,0:T(8,128)(2,1)}, u32[]{:S(2)}) copy-start(bf16[4,8,128]{2,1,0:T(8,128)(2,1)} %param.14) | copy-start | bytes 24580
  6.5 3.7 %copy-start.1 = (bf16[4,2,2,512,128]{4,3,2,1,0:T(8,128)(2,1)S(1)}, bf16[4,2,2,512,128]{4,3,2,1,0:T(8,128)(2,1)}, u32[]{:S(2)}) copy-start(bf16[4,2,2,512,128]{4,3,2,1,0:T(8,128)(2,1)} %param.15) | copy-start | bytes 6291460
  6.5 3.4 %copy-start.11 = (s32[32]{0:T(128)S(1)}, s32[32]{0:T(128)}, u32[]{:S(2)}) copy-start(s32[32]{0:T(128)} %param.19) | copy-start | bytes 388
  6.5 3.4 %copy-start.6 = (bf16[8,2,1024]{2,1,0:T(2,128)(2,1)S(1)}, bf16[8,2,1024]{2,1,0:T(2,128)(2,1)}, u32[]{:S(2)}) copy-start(bf16[8,2,1024]{2,1,0:T(2,128)(2,1)} %param.20) | copy-start | bytes 98308
  6.5 158.5 %reduce-scatter.2.cloned.1.call-start = ((), (), s32[]{:S(2)}) async-start(), calls=%async_computation.1 | async-start | bytes 589824 | tf_op jit(solution)/shard_map/reduce_scatter | solution.py:130
  10.3 32.6 %copy-start.9 = (s32[8,2]{0,1:T(2,128)S(1)}, s32[8,2]{0,1:T(2,128)}, u32[]{:S(2)}) copy-start(s32[8,2]{0,1:T(2,128)} %param.21) | copy-start | bytes 196
  47.4 1.7 copy-start.12
  49.5 6.7 %copy-start.5 = (bf16[32,2,1024]{2,1,0:T(2,128)(2,1)S(1)}, bf16[32,2,1024]{2,1,0:T(2,128)(2,1)}, u32[]{:S(2)}) copy-start(bf16[32,2,1024]{2,1,0:T(2,128)(2,1)} %param.25) | copy-start | bytes 393220
  49.5 6.7 %copy-start.7 = (s32[16,16]{1,0:T(8,128)S(1)}, s32[16,16]{1,0:T(8,128)}, u32[]{:S(2)}) copy-start(s32[16,16]{1,0:T(8,128)} %param.24) | copy-start | bytes 3076
  49.5 6.8 %copy-start.8 = (s32[16,16]{1,0:T(8,128)S(1)}, s32[16,16]{1,0:T(8,128)}, u32[]{:S(2)}) copy-start(s32[16,16]{1,0:T(8,128)} %param.23) | copy-start | bytes 3076
  50.4 10.5 %collective-permute-start = (bf16[16,16,1024]{2,0,1:T(8,128)(2,1)S(1)}, bf16[16,16,1024]{2,0,1:T(8,128)(2,1)S(1)}, u32[]{:S(2)}, u32[]{:S(2)}) collective-permute-start(bf16[16,16,1024]{2,0,1:T(8,128)(2,1)S(1)} %fusion.16), channel_id=1, source_target_pairs={{0,8},{8,16},{16,24},{24,32},{32,40},{40,48},{48,56},{56,64},{64,7... | collective-permute-start | bytes 1572872 | tf_op jit(solution)/shard_map/ppermute | solution.py:17
  52.3 10.3 %collective-permute-start.1 = (bf16[16,16,1024]{2,0,1:T(8,128)(2,1)S(1)}, bf16[16,16,1024]{2,0,1:T(8,128)(2,1)}, u32[]{:S(2)}, u32[]{:S(2)}) collective-permute-start(bf16[16,16,1024]{2,0,1:T(8,128)(2,1)S(1)} %fusion.16), channel_id=1, source_target_pairs={{8,0},{16,8},{24,16},{32,24},{40,32},{48,40},{56,48},{64,56},{72,6... | collective-permute-start | bytes 1572872 | tf_op jit(solution)/shard_map/ppermute | solution.py:19
  116.5 13.4 %copy-start.10 = (s32[4,8]{1,0:T(4,128)S(1)}, s32[4,8]{1,0:T(4,128)}, u32[]{:S(2)}) copy-start(s32[4,8]{1,0:T(4,128)} %param.17) | copy-start | bytes 388
  120.6 45.3 %copy-start.2 = (bf16[4,2,2,512,128]{4,3,2,1,0:T(8,128)(2,1)S(1)}, bf16[4,2,2,512,128]{4,3,2,1,0:T(8,128)(2,1)}, u32[]{:S(2)}) copy-start(bf16[4,2,2,512,128]{4,3,2,1,0:T(8,128)(2,1)} %param.15) | copy-start | bytes 6291460
  121.6 8.4 %collective-permute-start.2 = (bf16[4,8,128]{2,1,0:T(8,128)(2,1)S(1)}, bf16[4,8,128]{2,1,0:T(8,128)(2,1)S(1)}, u32[]{:S(2)}, u32[]{:S(2)}) collective-permute-start(bf16[4,8,128]{2,1,0:T(8,128)(2,1)S(1)} %copy-done.4), channel_id=1, source_target_pairs={{0,1},{1,2},{2,3},{3,4},{4,5},{5,6},{6,7},{7,8},{8,9},{9,10},{10,1... | collective-permute-start | bytes 24584 | tf_op jit(solution)/shard_map/ppermute | solution.py:17
  125.3 5.9 %collective-permute-start.3 = (bf16[4,8,128]{2,1,0:T(8,128)(2,1)S(1)}, bf16[4,8,128]{2,1,0:T(8,128)(2,1)S(1)}, u32[]{:S(2)}, u32[]{:S(2)}) collective-permute-start(bf16[4,8,128]{2,1,0:T(8,128)(2,1)S(1)} %copy-done.4), channel_id=1, source_target_pairs={{1,0},{2,1},{3,2},{4,3},{5,4},{6,5},{7,6},{8,7},{9,8},{10,9},{11,1... | collective-permute-start | bytes 24584 | tf_op jit(solution)/shard_map/ppermute | solution.py:19
  166.1 1.6 copy-start.3
Sparse Core Ops, SparseCore 0:
  121.7 43.2 reduce-scatter.1
where the time goes:
time: 177 us; the launch traced here: 176 us
  local copies, waits for them, and re-layouts  44.3 us (25%)
  waiting for transfers between devices  37.4 us (21%)
  blocking collectives  31.6 us (18%)
  matrix products  19.5 us (11%)
  other arithmetic  14.1 us (8%)
  starting transfers between devices  14 us (8%)
  between operations  13.8 us (8%)
    gather x16, local copies, waits for them, and re-layouts, add_entry(): jnp.take(padded, top_src[:, entry] - base_index, axis=0).astype(jnp.float32)  31.8 us
    all_gather x1, blocking collectives, per_device(): piece = lax.all_gather(patterns, 'samp', axis=0, tiled=True)  31.6 us
    reduce_scatter x1, waiting for transfers between devices, per_device(): lax.psum_scatter(folded.reshape(leaf_count * lax.axis_size('samp'), comps...  29.9 us
    dot_general x32, matrix products, contract(): jnp.einsum(form, first_op, second_op, preferred_element_type=jnp.float32)  14.6 us
    ppermute x2, starting transfers between devices, with_halo(): lax.ppermute(head, axis, [((i + 1) % count, i) for i in range(ends)])  8.4 us
    ppermute x2, starting transfers between devices, with_halo(): lax.ppermute(tail, axis, [(i, (i + 1) % count) for i in range(ends)])  5.61 us
    add x16, other arithmetic, add_entry(): return total + jnp.concatenate([part_real, part_imag], axis=1)  5.52 us
    ppermute x2, waiting for transfers between devices, with_halo(): lax.ppermute(tail, axis, [(i, (i + 1) % count) for i in range(ends)])  4.53 us
  transfers between devices with their start and end apart: 5, of which 4 were waited for; matrix products, arithmetic and copies ran while one was open for 2% of the time, Pallas kernels for 0%

commit v1 on v0

--- a/solution.py
+++ b/solution.py
@@ -4,6 +4,12 @@
 from jax.sharding import PartitionSpec as P
 
 HIGHEST = lax.Precision.HIGHEST
+
+
+def gather_from_all(x, axis, dim):
+    size = lax.axis_size(axis)
+    repeats = [size if d == dim else 1 for d in range(x.ndim)]
+    return lax.all_to_all(jnp.tile(x, repeats), axis, split_axis=dim, concat_axis=dim, tiled=True)
 
 
 def with_halo(cells, sides, width):
@@ -75,7 +81,7 @@
         ],
         axis=1,
     ).astype(jnp.bfloat16)
-    piece = lax.all_gather(patterns, "samp", axis=0, tiled=True)
+    piece = gather_from_all(patterns, "samp", 0)
     piece_rows = piece.shape[0]
     picked = piece.reshape(piece_rows, comps, in_blocks, block_size)[:, :, interp_idx, :]
     moved_rows = contract("lcbri,brki->lcbk", picked, interp_val)

time: 177 us -> 171 us (0.966)
  blocking collectives: 31.6 us -> 0 us
  waiting for transfers between devices: 37.4 us -> 52.1 us
  starting transfers between devices: 14 us -> 23.8 us
    all_gather x1 -> x0, blocking collectives: 31.6 us -> none  [per_device(): piece = lax.all_gather(patterns, 'samp', axis=0, tiled=True)]
    all_to_all x0 -> x1, waiting for transfers between devices: none -> 16.5 us  [gather_from_all(): lax.all_to_all(jnp.tile(x, repeats), axis, split_axis=dim, concat_axis=di...]
    all_to_all x0 -> x1, starting transfers between devices: none -> 10.3 us  [gather_from_all(): lax.all_to_all(jnp.tile(x, repeats), axis, split_axis=dim, concat_axis=di...]
    unnamed x32 -> x34, local copies, waits for them, and re-layouts: 3.28 us -> 3.62 us
  transfers between devices with their start and end apart: 5 -> 6, of which waited for: 4 -> 5; matrix products, arithmetic and copies ran while one was open for 2% -> 3% of each run, Pallas kernels for 0% -> 0%
where the time goes in v1:
time: 171 us; the launch traced here: 170 us
  waiting for transfers between devices  52.1 us (30%)
  local copies, waits for them, and re-layouts  45.5 us (27%)
  starting transfers between devices  23.8 us (14%)
  matrix products  19.4 us (11%)
  other arithmetic  14.5 us (8%)
  between operations  13.8 us (8%)
    gather x16, local copies, waits for them, and re-layouts, add_entry(): jnp.take(padded, top_src[:, entry] - base_index, axis=0).astype(jnp.float32)  31.8 us
    reduce_scatter x1, waiting for transfers between devices, per_device(): lax.psum_scatter(folded.reshape(leaf_count * lax.axis_size('samp'), comps...  28.2 us
    all_to_all x1, waiting for transfers between devices, gather_from_all(): lax.all_to_all(jnp.tile(x, repeats), axis, split_axis=dim, concat_axis=di...  16.5 us
    dot_general x32, matrix products, contract(): jnp.einsum(form, first_op, second_op, preferred_element_type=jnp.float32)  14.5 us
    all_to_all x1, starting transfers between devices, gather_from_all(): lax.all_to_all(jnp.tile(x, repeats), axis, split_axis=dim, concat_axis=di...  10.3 us
    ppermute x2, starting transfers between devices, with_halo(): lax.ppermute(head, axis, [((i + 1) % count, i) for i in range(ends)])  9.02 us
    add x16, other arithmetic, add_entry(): return total + jnp.concatenate([part_real, part_imag], axis=1)  5.52 us
    ppermute x2, waiting for transfers between devices, with_halo(): lax.ppermute(tail, axis, [(i, (i + 1) % count) for i in range(ends)])  4.53 us
  transfers between devices with their start and end apart: 6, of which 5 were waited for; matrix products, arithmetic and copies ran while one was open for 3% of the time, Pallas kernels for 0%

profile of v1, /device:TPU:2, one launch (start us, length us, event | category | flops | bytes accessed | tf_op | source)
XLA Modules:
  0.0 170.4 jit_solution(2698245693902373581)
XLA Ops:
  6.5 1.8 %fusion.46 = f32[4,4,2,512]{3,1,2,0:T(4,128)S(1)} fusion(bf16[4,2,2,512,128]{4,3,2,1,0:T(8,128)(2,1)} %param.15, bf16[4,8,128]{2,1,0:T(8,128)(2,1)} %param.14), kind=kOutput, calls=%fused_computation.65 | convolution fusion | flops 4194304 | bytes 1118208 | tf_op jit(solution)/shard_map/lpqu,leu->lpeq/dot_general | solution.py:37
  8.3 1.6 fusion.44
  10.8 0.9 tile.4
  11.7 10.3 %all-to-all-start = ((bf16[32,16,512]{2,1,0:T(8,128)(2,1)}), bf16[32,16,512]{2,1,0:T(8,128)(2,1)S(1)}, u32[]{:S(2)}, u32[]{:S(2)}) async-start(bf16[32,16,512]{2,1,0:T(8,128)(2,1)} %bitcast.15), calls=%async_computation | async-start | bytes 1048576 | tf_op jit(solution)/shard_map/all_to_all | solution.py:12
  22.3 0.5 broadcast_subtract_fusion
  23.1 16.5 %all-to-all-done = bf16[32,16,512]{2,1,0:T(8,128)(2,1)S(1)} async-done(((bf16[32,16,512]{2,1,0:T(8,128)(2,1)}), bf16[32,16,512]{2,1,0:T(8,128)(2,1)S(1)}, u32[]{:S(2)}, u32[]{:S(2)}) %all-to-all-start) | async-done | bytes 524320 | tf_op jit(solution)/shard_map/all_to_all | solution.py:12
  39.6 1.1 gather_fusion.1
  40.7 0.7 convolution_bitcast_fusion.1
  41.4 2.6 %copy.73 = f32[32,16,8,128]{3,2,0,1:T(8,128)} copy(f32[32,16,8,128]{3,1,0,2:T(8,128)S(1)} %convolution_bitcast_fusion.1) | data formatting | bytes 4194304 | tf_op jit(solution)/shard_map/reshape | solution.py:88
  44.0 1.7 %reshape.110 = f32[32,16,1024]{2,0,1:T(8,128)S(1)} reshape(f32[32,16,8,128]{3,2,0,1:T(8,128)} %copy.73) | data formatting | bytes 4194304 | tf_op jit(solution)/shard_map/reshape | solution.py:88
  46.3 0.8 fusion.16
  47.2 1.9 %collective-permute-start = (bf16[16,16,1024]{2,0,1:T(8,128)(2,1)S(1)}, bf16[16,16,1024]{2,0,1:T(8,128)(2,1)S(1)}, u32[]{:S(2)}, u32[]{:S(2)}) collective-permute-start(bf16[16,16,1024]{2,0,1:T(8,128)(2,1)S(1)} %fusion.16), channel_id=1, source_target_pairs={{0,8},{8,16},{16,24},{24,32},{32,40},{40,48},{48,56},{56,64},{64,7... | collective-permute-start | bytes 1572872 | tf_op jit(solution)/shard_map/ppermute | solution.py:23
  49.1 3.8 %collective-permute-start.1 = (bf16[16,16,1024]{2,0,1:T(8,128)(2,1)S(1)}, bf16[16,16,1024]{2,0,1:T(8,128)(2,1)}, u32[]{:S(2)}, u32[]{:S(2)}) collective-permute-start(bf16[16,16,1024]{2,0,1:T(8,128)(2,1)S(1)} %fusion.16), channel_id=1, source_target_pairs={{8,0},{16,8},{24,16},{32,24},{40,32},{48,40},{56,48},{64,56},{72,6... | collective-permute-start | bytes 1572872 | tf_op jit(solution)/shard_map/ppermute | solution.py:25
  53.1 4.5 %collective-permute-done = bf16[16,16,1024]{2,0,1:T(8,128)(2,1)S(1)} collective-permute-done((bf16[16,16,1024]{2,0,1:T(8,128)(2,1)S(1)}, bf16[16,16,1024]{2,0,1:T(8,128)(2,1)S(1)}, u32[]{:S(2)}, u32[]{:S(2)}) %collective-permute-start) | collective-permute-done | bytes 524320 | tf_op jit(solution)/shard_map/ppermute | solution.py:23
  57.7 1.8 %collective-permute-done.1 = bf16[16,16,1024]{2,0,1:T(8,128)(2,1)} collective-permute-done((bf16[16,16,1024]{2,0,1:T(8,128)(2,1)S(1)}, bf16[16,16,1024]{2,0,1:T(8,128)(2,1)}, u32[]{:S(2)}, u32[]{:S(2)}) %collective-permute-start.1) | collective-permute-done | bytes 524320 | tf_op jit(solution)/shard_map/ppermute | solution.py:25
  59.4 1.2 pad_maximum_fusion
  60.6 2.1 %copy.51 = bf16[48,16,1024]{2,1,0:T(8,128)(2,1)} copy(bf16[48,16,1024]{2,0,1:T(8,128)(2,1)S(1)} %pad_maximum_fusion) | data formatting | bytes 3145728
  62.7 48.1 %while.14 = (s32[]{:T(128)}, f32[16,16,1024]{2,1,0:T(8,128)S(1)}, s32[16,16]{0,1:T(8,128)S(1)}, bf16[32,2,1024]{2,0,1:T(8,128)(2,1)S(1)}, s32[16,16]{0,1:T(8,128...) while((s32[]{:T(128)}, f32[16,16,1024]{2,1,0:T(8,128)S(1)}, ...), condition=%wide.region_1.0_spmd.clone, body=%wide.region_0.1_spmd.clone.sunk | while | flops 4195955 | bytes 8524371 | solution.py:119
  62.7 2.0 %gather_fusion = bf16[16,16,1024]{2,1,0:T(8,128)(2,1)S(1)} fusion(bf16[48,16,1024]{2,1,0:T(8,128)(2,1)} %get-tuple-element.285, s32[1024]{0:T(1024)S(1)} %pad_clamp_fusion.4), kind=kCustom, calls=%fused_computation.clone.clone.1 | custom fusion | bytes 1048640 | tf_op jit(solution)/shard_map/while/body/eval_jaxpr/jit(_take)/gather | solution.py:109
  65.7 2.0 %gather_fusion = bf16[16,16,1024]{2,1,0:T(8,128)(2,1)S(1)} fusion(bf16[48,16,1024]{2,1,0:T(8,128)(2,1)} %get-tuple-element.285, s32[1024]{0:T(1024)S(1)} %pad_clamp_fusion.4), kind=kCustom, calls=%fused_computation.clone.clone.1 | custom fusion | bytes 1048640 | tf_op jit(solution)/shard_map/while/body/eval_jaxpr/jit(_take)/gather | solution.py:109
  68.7 2.0 %gather_fusion = bf16[16,16,1024]{2,1,0:T(8,128)(2,1)S(1)} fusion(bf16[48,16,1024]{2,1,0:T(8,128)(2,1)} %get-tuple-element.285, s32[1024]{0:T(1024)S(1)} %pad_clamp_fusion.4), kind=kCustom, calls=%fused_computation.clone.clone.1 | custom fusion | bytes 1048640 | tf_op jit(solution)/shard_map/while/body/eval_jaxpr/jit(_take)/gather | solution.py:109
  71.7 2.0 %gather_fusion = bf16[16,16,1024]{2,1,0:T(8,128)(2,1)S(1)} fusion(bf16[48,16,1024]{2,1,0:T(8,128)(2,1)} %get-tuple-element.285, s32[1024]{0:T(1024)S(1)} %pad_clamp_fusion.4), kind=kCustom, calls=%fused_computation.clone.clone.1 | custom fusion | bytes 1048640 | tf_op jit(solution)/shard_map/while/body/eval_jaxpr/jit(_take)/gather | solution.py:109
  74.7 2.0 %gather_fusion = bf16[16,16,1024]{2,1,0:T(8,128)(2,1)S(1)} fusion(bf16[48,16,1024]{2,1,0:T(8,128)(2,1)} %get-tuple-element.285, s32[1024]{0:T(1024)S(1)} %pad_clamp_fusion.4), kind=kCustom, calls=%fused_computation.clone.clone.1 | custom fusion | bytes 1048640 | tf_op jit(solution)/shard_map/while/body/eval_jaxpr/jit(_take)/gather | solution.py:109
  77.7 2.0 %gather_fusion = bf16[16,16,1024]{2,1,0:T(8,128)(2,1)S(1)} fusion(bf16[48,16,1024]{2,1,0:T(8,128)(2,1)} %get-tuple-element.285, s32[1024]{0:T(1024)S(1)} %pad_clamp_fusion.4), kind=kCustom, calls=%fused_computation.clone.clone.1 | custom fusion | bytes 1048640 | tf_op jit(solution)/shard_map/while/body/eval_jaxpr/jit(_take)/gather | solution.py:109
  80.7 2.0 %gather_fusion = bf16[16,16,1024]{2,1,0:T(8,128)(2,1)S(1)} fusion(bf16[48,16,1024]{2,1,0:T(8,128)(2,1)} %get-tuple-element.285, s32[1024]{0:T(1024)S(1)} %pad_clamp_fusion.4), kind=kCustom, calls=%fused_computation.clone.clone.1 | custom fusion | bytes 1048640 | tf_op jit(solution)/shard_map/while/body/eval_jaxpr/jit(_take)/gather | solution.py:109
  83.7 2.0 %gather_fusion = bf16[16,16,1024]{2,1,0:T(8,128)(2,1)S(1)} fusion(bf16[48,16,1024]{2,1,0:T(8,128)(2,1)} %get-tuple-element.285, s32[1024]{0:T(1024)S(1)} %pad_clamp_fusion.4), kind=kCustom, calls=%fused_computation.clone.clone.1 | custom fusion | bytes 1048640 | tf_op jit(solution)/shard_map/while/body/eval_jaxpr/jit(_take)/gather | solution.py:109
  86.7 2.0 %gather_fusion = bf16[16,16,1024]{2,1,0:T(8,128)(2,1)S(1)} fusion(bf16[48,16,1024]{2,1,0:T(8,128)(2,1)} %get-tuple-element.285, s32[1024]{0:T(1024)S(1)} %pad_clamp_fusion.4), kind=kCustom, calls=%fused_computation.clone.clone.1 | custom fusion | bytes 1048640 | tf_op jit(solution)/shard_map/while/body/eval_jaxpr/jit(_take)/gather | solution.py:109
  89.7 2.0 %gather_fusion = bf16[16,16,1024]{2,1,0:T(8,128)(2,1)S(1)} fusion(bf16[48,16,1024]{2,1,0:T(8,128)(2,1)} %get-tuple-element.285, s32[1024]{0:T(1024)S(1)} %pad_clamp_fusion.4), kind=kCustom, calls=%fused_computation.clone.clone.1 | custom fusion | bytes 1048640 | tf_op jit(solution)/shard_map/while/body/eval_jaxpr/jit(_take)/gather | solution.py:109
  92.7 2.0 %gather_fusion = bf16[16,16,1024]{2,1,0:T(8,128)(2,1)S(1)} fusion(bf16[48,16,1024]{2,1,0:T(8,128)(2,1)} %get-tuple-element.285, s32[1024]{0:T(1024)S(1)} %pad_clamp_fusion.4), kind=kCustom, calls=%fused_computation.clone.clone.1 | custom fusion | bytes 1048640 | tf_op jit(solution)/shard_map/while/body/eval_jaxpr/jit(_take)/gather | solution.py:109
  95.7 2.0 %gather_fusion = bf16[16,16,1024]{2,1,0:T(8,128)(2,1)S(1)} fusion(bf16[48,16,1024]{2,1,0:T(8,128)(2,1)} %get-tuple-element.285, s32[1024]{0:T(1024)S(1)} %pad_clamp_fusion.4), kind=kCustom, calls=%fused_computation.clone.clone.1 | custom fusion | bytes 1048640 | tf_op jit(solution)/shard_map/while/body/eval_jaxpr/jit(_take)/gather | solution.py:109
  98.8 2.0 %gather_fusion = bf16[16,16,1024]{2,1,0:T(8,128)(2,1)S(1)} fusion(bf16[48,16,1024]{2,1,0:T(8,128)(2,1)} %get-tuple-element.285, s32[1024]{0:T(1024)S(1)} %pad_clamp_fusion.4), kind=kCustom, calls=%fused_computation.clone.clone.1 | custom fusion | bytes 1048640 | tf_op jit(solution)/shard_map/while/body/eval_jaxpr/jit(_take)/gather | solution.py:109
  101.8 2.0 %gather_fusion = bf16[16,16,1024]{2,1,0:T(8,128)(2,1)S(1)} fusion(bf16[48,16,1024]{2,1,0:T(8,128)(2,1)} %get-tuple-element.285, s32[1024]{0:T(1024)S(1)} %pad_clamp_fusion.4), kind=kCustom, calls=%fused_computation.clone.clone.1 | custom fusion | bytes 1048640 | tf_op jit(solution)/shard_map/while/body/eval_jaxpr/jit(_take)/gather | solution.py:109
  104.8 2.0 %gather_fusion = bf16[16,16,1024]{2,1,0:T(8,128)(2,1)S(1)} fusion(bf16[48,16,1024]{2,1,0:T(8,128)(2,1)} %get-tuple-element.285, s32[1024]{0:T(1024)S(1)} %pad_clamp_fusion.4), kind=kCustom, calls=%fused_computation.clone.clone.1 | custom fusion | bytes 1048640 | tf_op jit(solution)/shard_map/while/body/eval_jaxpr/jit(_take)/gather | solution.py:109
  107.8 2.0 %gather_fusion = bf16[16,16,1024]{2,1,0:T(8,128)(2,1)S(1)} fusion(bf16[48,16,1024]{2,1,0:T(8,128)(2,1)} %get-tuple-element.285, s32[1024]{0:T(1024)S(1)} %pad_clamp_fusion.4), kind=kCustom, calls=%fused_computation.clone.clone.1 | custom fusion | bytes 1048640 | tf_op jit(solution)/shard_map/while/body/eval_jaxpr/jit(_take)/gather | solution.py:109
  110.8 0.5 fusion.62
  112.6 0.7 convolution_bitcast_fusion
  113.3 4.1 %fusion.19 = bf16[32,16,4,128]{3,2,1,0:T(4,128)(2,1)S(1)} fusion(f32[32,16,8,2,128]{4,1,3,0,2:T(8,128)S(1)} %convolution_bitcast_fusion, s32[8,2]{0,1:T(2,128)S(1)} %copy-done.9), kind=kOutput, calls=%fused_computation.29 | convolution fusion | flops 50593856 | bytes 4718656 | tf_op jit(solution)/shard_map/lcbri,brq->lcqi/dot_general | solution.py:135
  117.4 1.0 convert_element_type.40
  118.4 2.5 %collective-permute-start.2 = (bf16[4,8,128]{2,1,0:T(8,128)(2,1)S(1)}, bf16[4,8,128]{2,1,0:T(8,128)(2,1)S(1)}, u32[]{:S(2)}, u32[]{:S(2)}) collective-permute-start(bf16[4,8,128]{2,1,0:T(8,128)(2,1)S(1)} %copy-done.4), channel_id=1, source_target_pairs={{0,1},{1,2},{2,3},{3,4},{4,5},{5,6},{6,7},{7,8},{8,9},{9,10},{10,1... | collective-permute-start | bytes 24584 | tf_op jit(solution)/shard_map/ppermute | solution.py:23
  120.9 5.2 %collective-permute-start.3 = (bf16[4,8,128]{2,1,0:T(8,128)(2,1)S(1)}, bf16[4,8,128]{2,1,0:T(8,128)(2,1)S(1)}, u32[]{:S(2)}, u32[]{:S(2)}) collective-permute-start(bf16[4,8,128]{2,1,0:T(8,128)(2,1)S(1)} %copy-done.4), channel_id=1, source_target_pairs={{1,0},{2,1},{3,2},{4,3},{5,4},{6,5},{7,6},{8,7},{9,8},{10,9},{11,1... | collective-permute-start | bytes 24584 | tf_op jit(solution)/shard_map/ppermute | solution.py:25
  126.2 1.2 collective-permute-done.3
  127.4 0.6 gather_fusion.2
  128.1 1.6 convolution_bitcast_fusion.7
  129.7 1.6 convolution_bitcast_fusion.3
  131.4 28.2 %reduce-scatter.2.cloned.1.call-done = bf16[4,16,512]{2,1,0:T(8,128)(2,1)} async-done(((bf16[32,16,512]{2,1,0:T(8,128)(2,1)}), bf16[4,16,512]{2,1,0:T(8,128)(2,1)}) %reduce-scatter.2.cloned.1.call-update) | async-done | bytes 65552 | tf_op jit(solution)/shard_map/reduce_scatter | solution.py:136
  159.5 0.8 fusion.91
  161.4 0.8 copy-done.3
  162.9 0.6 pad_maximum_fusion.3
  (194 shorter events, 20.6 us)
Async XLA Ops:
  6.5 34.2 %copy-start = (bf16[8,2,128,128]{3,2,1,0:T(8,128)(2,1)S(1)}, bf16[8,2,128,128]{3,2,1,0:T(8,128)(2,1)}, u32[]{:S(2)}) copy-start(bf16[8,2,128,128]{3,2,1,0:T(8,128)(2,1)} %param.22) | copy-start | bytes 1572868
  6.5 3.4 %copy-start.4 = (bf16[4,8,128]{2,1,0:T(8,128)(2,1)S(1)}, bf16[4,8,128]{2,1,0:T(8,128)(2,1)}, u32[]{:S(2)}) copy-start(bf16[4,8,128]{2,1,0:T(8,128)(2,1)} %param.14) | copy-start | bytes 24580
  6.5 3.4 %copy-start.1 = (bf16[4,2,2,512,128]{4,3,2,1,0:T(8,128)(2,1)S(1)}, bf16[4,2,2,512,128]{4,3,2,1,0:T(8,128)(2,1)}, u32[]{:S(2)}) copy-start(bf16[4,2,2,512,128]{4,3,2,1,0:T(8,128)(2,1)} %param.15) | copy-start | bytes 6291460
  9.9 12.1 %copy-start.9 = (s32[8,2]{0,1:T(2,128)S(1)}, s32[8,2]{0,1:T(2,128)}, u32[]{:S(2)}) copy-start(s32[8,2]{0,1:T(2,128)} %param.21) | copy-start | bytes 196
  10.0 12.3 %copy-start.13 = (s32[32]{0:T(128)S(1)}, s32[32]{0:T(128)}, u32[]{:S(2)}) copy-start(s32[32]{0:T(128)} %param.18) | copy-start | bytes 388
  10.0 12.8 %copy-start.6 = (bf16[8,2,1024]{2,1,0:T(2,128)(2,1)S(1)}, bf16[8,2,1024]{2,1,0:T(2,128)(2,1)}, u32[]{:S(2)}) copy-start(bf16[8,2,1024]{2,1,0:T(2,128)(2,1)} %param.20) | copy-start | bytes 98308
  10.0 12.8 %copy-start.12 = (s32[32]{0:T(128)S(1)}, s32[32]{0:T(128)}, u32[]{:S(2)}) copy-start(s32[32]{0:T(128)} %param.19) | copy-start | bytes 388
  11.7 27.8 %all-to-all-start = ((bf16[32,16,512]{2,1,0:T(8,128)(2,1)}), bf16[32,16,512]{2,1,0:T(8,128)(2,1)S(1)}, u32[]{:S(2)}, u32[]{:S(2)}) async-start(bf16[32,16,512]{2,1,0:T(8,128)(2,1)} %bitcast.15), calls=%async_computation | async-start | bytes 1048576 | tf_op jit(solution)/shard_map/all_to_all | solution.py:12
  22.0 137.5 %reduce-scatter.2.cloned.1.call-start = ((), (), s32[]{:S(2)}) async-start(), calls=%async_computation.2 | async-start | bytes 589824 | tf_op jit(solution)/shard_map/reduce_scatter | solution.py:136
  45.7 0.7 copy-start.11
  46.0 7.0 %copy-start.5 = (bf16[32,2,1024]{2,1,0:T(2,128)(2,1)S(1)}, bf16[32,2,1024]{2,1,0:T(2,128)(2,1)}, u32[]{:S(2)}) copy-start(bf16[32,2,1024]{2,1,0:T(2,128)(2,1)} %param.25) | copy-start | bytes 393220
  46.0 7.0 %copy-start.7 = (s32[16,16]{1,0:T(8,128)S(1)}, s32[16,16]{1,0:T(8,128)}, u32[]{:S(2)}) copy-start(s32[16,16]{1,0:T(8,128)} %param.24) | copy-start | bytes 3076
  46.0 7.1 %copy-start.8 = (s32[16,16]{1,0:T(8,128)S(1)}, s32[16,16]{1,0:T(8,128)}, u32[]{:S(2)}) copy-start(s32[16,16]{1,0:T(8,128)} %param.23) | copy-start | bytes 3076
  47.2 10.5 %collective-permute-start = (bf16[16,16,1024]{2,0,1:T(8,128)(2,1)S(1)}, bf16[16,16,1024]{2,0,1:T(8,128)(2,1)S(1)}, u32[]{:S(2)}, u32[]{:S(2)}) collective-permute-start(bf16[16,16,1024]{2,0,1:T(8,128)(2,1)S(1)} %fusion.16), channel_id=1, source_target_pairs={{0,8},{8,16},{16,24},{24,32},{32,40},{40,48},{48,56},{56,64},{64,7... | collective-permute-start | bytes 1572872 | tf_op jit(solution)/shard_map/ppermute | solution.py:23
  49.1 10.3 %collective-permute-start.1 = (bf16[16,16,1024]{2,0,1:T(8,128)(2,1)S(1)}, bf16[16,16,1024]{2,0,1:T(8,128)(2,1)}, u32[]{:S(2)}, u32[]{:S(2)}) collective-permute-start(bf16[16,16,1024]{2,0,1:T(8,128)(2,1)S(1)} %fusion.16), channel_id=1, source_target_pairs={{8,0},{16,8},{24,16},{32,24},{40,32},{48,40},{56,48},{64,56},{72,6... | collective-permute-start | bytes 1572872 | tf_op jit(solution)/shard_map/ppermute | solution.py:25
  113.3 12.8 %copy-start.10 = (s32[4,8]{1,0:T(4,128)S(1)}, s32[4,8]{1,0:T(4,128)}, u32[]{:S(2)}) copy-start(s32[4,8]{1,0:T(4,128)} %param.17) | copy-start | bytes 388
  117.4 43.0 %copy-start.2 = (bf16[4,2,2,512,128]{4,3,2,1,0:T(8,128)(2,1)S(1)}, bf16[4,2,2,512,128]{4,3,2,1,0:T(8,128)(2,1)}, u32[]{:S(2)}) copy-start(bf16[4,2,2,512,128]{4,3,2,1,0:T(8,128)(2,1)} %param.15) | copy-start | bytes 6291460
  118.4 7.8 %collective-permute-start.2 = (bf16[4,8,128]{2,1,0:T(8,128)(2,1)S(1)}, bf16[4,8,128]{2,1,0:T(8,128)(2,1)S(1)}, u32[]{:S(2)}, u32[]{:S(2)}) collective-permute-start(bf16[4,8,128]{2,1,0:T(8,128)(2,1)S(1)} %copy-done.4), channel_id=1, source_target_pairs={{0,1},{1,2},{2,3},{3,4},{4,5},{5,6},{6,7},{7,8},{8,9},{9,10},{10,1... | collective-permute-start | bytes 24584 | tf_op jit(solution)/shard_map/ppermute | solution.py:23
  120.9 6.6 %collective-permute-start.3 = (bf16[4,8,128]{2,1,0:T(8,128)(2,1)S(1)}, bf16[4,8,128]{2,1,0:T(8,128)(2,1)S(1)}, u32[]{:S(2)}, u32[]{:S(2)}) collective-permute-start(bf16[4,8,128]{2,1,0:T(8,128)(2,1)S(1)} %copy-done.4), channel_id=1, source_target_pairs={{1,0},{2,1},{3,2},{4,3},{5,4},{6,5},{7,6},{8,7},{9,8},{10,9},{11,1... | collective-permute-start | bytes 24584 | tf_op jit(solution)/shard_map/ppermute | solution.py:25
  160.6 1.6 copy-start.3
Sparse Core Ops, SparseCore 0:
  118.5 40.9 reduce-scatter.1
